TPU v7x, 32 devices: a whole 2x2x4 slice. The times are simulated.
32 devices in a mesh: row: 8 (over z, x), col: 2 (over core), rank: 2 (over y).
Axes of the slice: x: 2, y: 2, z: 4, core: 2. Of those that a mesh axis runs over, the one named last changes fastest.
Arguments:
- tensor: bfloat16 [64, 2048, 2048], P(None, 'row', 'col'), may hold values from -6 to 6
- aux_factor: bfloat16 [64, 256], P(None, 'rank'), may hold values from -0.75 to 0.75
- row_factor: bfloat16 [2048, 256], P(('row', 'col'), 'rank'), may hold values from -0.125 to 0.125
- col_factor: bfloat16 [2048, 256], P(('col', 'row'), 'rank'), may hold values from -0.125 to 0.125
Outputs:
- row_result: float32 [2048, 256], P(('row', 'col'), 'rank')
- aux_result: float32 [64, 256], P('row', 'rank')
All inputs are finite; a program needn't handle non-finite values.
Results may differ from a plain program's by a relative error of at most 0.0003.
Values may be sent and summed in bfloat16 or wider, within the bound.
A program may use at most 128 MiB of HBM per device.

v0:
```python
import jax
import jax.numpy as jnp
from jax import lax
from jax.sharding import PartitionSpec as P


def reduce_inner(inner, aux_factor, row_panel):
    aux_panel = aux_factor.astype(jnp.float32)
    aux_count = inner.shape[0]
    row_total = jnp.zeros((inner.shape[1], inner.shape[2]), jnp.float32)
    pieces = []
    for start in range(0, aux_count, 8):
        block = inner[start : start + 8]
        row_total = row_total + jnp.sum(block * aux_panel[start : start + 8][:, None, :], axis=0)
        pieces.append(jnp.sum(block * row_panel[None, :, :], axis=1))
    return (row_total, jnp.concatenate(pieces, axis=0))


def body(tensor, aux_factor, row_factor, col_factor):
    row_panel = lax.all_gather(row_factor, "col", axis=0, tiled=True).astype(jnp.float32)
    width = aux_factor.shape[1]
    aux_count = tensor.shape[0]
    orbits = tensor.shape[1]
    flat = tensor.reshape(aux_count * orbits, tensor.shape[2])
    columns = lax.all_gather(col_factor, "row", axis=0, tiled=True)
    inner = jnp.dot(flat, columns, preferred_element_type=jnp.float32)
    inner = inner.reshape(aux_count, orbits, width)
    row_total, aux_total = reduce_inner(inner, aux_factor, row_panel)
    row_result = lax.psum_scatter(row_total, "col", scatter_dimension=0, tiled=True)
    scattered = lax.psum_scatter(aux_total, "row", scatter_dimension=0, tiled=True)
    aux_result = lax.psum(scattered, "col")
    return (row_result, aux_result)


def solution(mesh):
    return jax.shard_map(
        body,
        mesh=mesh,
        in_specs=(
            P(None, "row", "col"),
            P(None, "rank"),
            P(("row", "col"), "rank"),
            P(("col", "row"), "rank"),
        ),
        out_specs=(P(("row", "col"), "rank"), P("row", "rank")),
        check_vma=False,
    )
```

profile of v0, /device:TPU:0, one launch (start us, length us, event | category | flops | bytes accessed | tf_op | source)
XLA Modules:
  0.0 115.6 jit_solution(7216242594102125668)
XLA Ops:
  7.2 0.0 reduce-scatter.2.cloned.1.call-start
  7.2 0.8 fusion.1
  8.0 32.8 %all_gather.6 = bf16[1024,128]{1,0:T(8,128)(2,1)S(1)} all-gather(bf16[128,128]{1,0:T(8,128)(2,1)} %param.7), channel_id=1, replica_groups=mesh['row'=8,'col'=2,'rank'=2] {'row'}, dimensions={0}, use_global_device_ids=true | all-gather | bytes 294912 | tf_op jit(solution)/shard_map/all_gather | solution.py:25
  40.8 0.0 copy-start.1
  40.8 0.0 copy-start.2
  40.8 14.9 %fusion.2 = f32[16384,128]{1,0:T(8,128)S(1)} fusion(bf16[16384,1024]{1,0:T(8,128)(2,1)} %bitcast.20, bf16[1024,128]{1,0:T(8,128)(2,1)S(1)} %all_gather.6), kind=kOutput, calls=%fused_computation.28 | convolution fusion | flops 4294967296 | bytes 42205184 | tf_op jit(solution)/shard_map/dot_general | solution.py:26
  55.7 0.0 copy-start
  55.7 3.2 %copy-done = f32[16384,128]{1,0:T(8,128)} copy-done((f32[16384,128]{1,0:T(8,128)}, f32[16384,128]{1,0:T(8,128)S(1)}, u32[]{:S(2)}) %copy-start) | copy-done | bytes 8388632
  58.9 0.6 fusion
  59.5 0.2 multiply_reduce_fusion.14
  59.6 0.2 multiply_reduce_fusion.8
  59.8 0.2 multiply_reduce_fusion.10
  59.9 0.2 multiply_reduce_fusion.12
  60.1 0.7 add_add_fusion
  60.8 0.0 reduce-scatter.2.cloned.1.call-update
  60.8 0.0 copy-done.1
  60.8 1.9 %all_gather.7 = bf16[256,128]{1,0:T(8,128)(2,1)S(1)} all-gather(bf16[128,128]{1,0:T(8,128)(2,1)S(1)} %copy-done.1), channel_id=1, replica_groups=mesh['row'=8,'col'=2,'rank'=2] {'col'}, dimensions={0}, use_global_device_ids=true | all-gather | bytes 98304 | tf_op jit(solution)/shard_map/all_gather | solution.py:20
  62.7 4.6 %multiply_reduce_fusion = (f32[8,128]{1,0:T(8,128)S(1)}, f32[8,128]{1,0:T(8,128)S(1)}, f32[8,128]{1,0:T(8,128)S(1)}, f32[8,128]{1,0:T(8,128)S(1)}, f32[8,128]{1,...) fusion(f32[256,128]{1,0:T(8,128)S(1)} %convert_element_type.7, f32[16384,128]{1,0:T(8,128)} %copy-done), kind=kLoop, calls=%fused_computation | loop fusion | flops 4186112 | bytes 8552448 | tf_op jit(solution)/shard_map/reduce_sum | solution.py:15
  67.4 0.0 copy-done.2
  67.4 0.6 dynamic-slice
  68.6 37.1 %all-reduce = f32[64,128]{1,0:T(8,128)S(1)} all-reduce(f32[64,128]{1,0:T(8,128)S(1)} %constant_dynamic-update-slice_fusion), channel_id=3, replica_groups=mesh['row'=8,'col'=2,'rank'=2] {'row'}, use_global_device_ids=true, to_apply=%region_17.0.clone | all-reduce | flops 8192 | bytes 65536
  105.7 3.0 %psum.7 = f32[8,128]{1,0:T(8,128)} all-reduce(f32[8,128]{1,0:T(8,128)S(1)} %constant_dynamic-slice_fusion), channel_id=1, replica_groups=mesh['row'=8,'col'=2,'rank'=2] {'col'}, use_global_device_ids=true, to_apply=%region_18.0 | all-reduce | flops 1024 | bytes 8192 | tf_op jit(solution)/shard_map/psum | solution.py:31
  108.8 0.0 reduce-scatter.2.cloned.1.call-done
  (10 shorter events, 0.0 us)
Async XLA Ops:
  7.2 101.6 %reduce-scatter.2.cloned.1.call-start = ((), (), s32[]{:S(2)}) async-start(), calls=%async_computation.1 | async-start | bytes 196608 | tf_op jit(solution)/shard_map/reduce_scatter | solution.py:29
  40.8 20.1 %copy-start.1 = (bf16[128,128]{1,0:T(8,128)(2,1)S(1)}, bf16[128,128]{1,0:T(8,128)(2,1)}, u32[]{:S(2)}) copy-start(bf16[128,128]{1,0:T(8,128)(2,1)} %param.6) | copy-start | bytes 98308
  40.8 26.6 %copy-start.2 = (u32[32]{0:T(128)S(1)}, u32[32]{0:T(128)}, u32[]{:S(2)}) copy-start(u32[32]{0:T(128)} %constant.4) | copy-start | bytes 388
  55.7 3.2 %copy-start = (f32[16384,128]{1,0:T(8,128)}, f32[16384,128]{1,0:T(8,128)S(1)}, u32[]{:S(2)}) copy-start(f32[16384,128]{1,0:T(8,128)S(1)} %fusion.2) | copy-start | bytes 25165828
Sparse Core Ops, SparseCore 0:
  61.0 8.5 reduce-scatter.1
where the time goes:
time: 116 us
  blocking collectives  74.7 us (64%)
  matrix products  14.9 us (13%)
  between operations  14.8 us (13%)
  other arithmetic  5.94 us (5%)
  local copies, waits for them, and re-layouts  5.2 us (4%)
    unnamed x1, blocking collectives  37.1 us
    all_gather x1, blocking collectives, body(): columns = lax.all_gather(col_factor, 'row', axis=0, tiled=True)  32.8 us
    dot_general x1, matrix products, body(): inner = jnp.dot(flat, columns, preferred_element_type=jnp.float32)  14.9 us
    reduce_sum x1, other arithmetic, reduce_inner(): pieces.append(jnp.sum(block * row_panel[None, :, :], axis=1))  4.59 us
    unnamed x15, local copies, waits for them, and re-layouts  3.83 us
    psum x1, blocking collectives, body(): aux_result = lax.psum(scattered, 'col')  3.04 us
  transfers between devices with their start and end apart: 1, of which 0 were waited for; matrix products, arithmetic and copies ran while one was open for 5% of the time, Pallas kernels for 0%

commit v1 on v0

--- a/solution.py
+++ b/solution.py
@@ -2,6 +2,28 @@
 import jax.numpy as jnp
 from jax import lax
 from jax.sharding import PartitionSpec as P
+
+
+def joined_along(tiles, dim):
+    tiles = jnp.moveaxis(tiles, 0, dim)
+    shape = tiles.shape
+    return tiles.reshape(*shape[:dim], shape[dim] * shape[dim + 1], *shape[dim + 2 :])
+
+
+def doubled(x, axis):
+    count = lax.axis_size(axis)
+    blocks = x[None]
+    for level in range(count.bit_length() - 1):
+        bit = 1 << level
+        other = lax.ppermute(blocks, axis, [(i, i ^ bit) for i in range(count)])
+        both = jnp.stack([blocks, other])
+        upper = lax.axis_index(axis) >> level & 1
+        blocks = jnp.where(upper == 0, both, both[::-1]).reshape(-1, *x.shape)
+    return blocks
+
+
+def gather_by_bits(x, axis, dim):
+    return joined_along(doubled(x, axis), dim)
 
 
 def reduce_inner(inner, aux_factor, row_panel):
@@ -22,7 +44,7 @@
     aux_count = tensor.shape[0]
     orbits = tensor.shape[1]
     flat = tensor.reshape(aux_count * orbits, tensor.shape[2])
-    columns = lax.all_gather(col_factor, "row", axis=0, tiled=True)
+    columns = gather_by_bits(col_factor, "row", 0)
     inner = jnp.dot(flat, columns, preferred_element_type=jnp.float32)
     inner = inner.reshape(aux_count, orbits, width)
     row_total, aux_total = reduce_inner(inner, aux_factor, row_panel)

time: 116 us -> 110 us (0.948)
  blocking collectives: 74.7 us -> 41.5 us
  local copies, waits for them, and re-layouts: 5.2 us -> 15 us
  starting transfers between devices: 0.04 us -> 8.34 us
  matrix products: 14.9 us -> 19 us
  other arithmetic: 5.94 us -> 8.59 us
  waiting for transfers between devices: 0.02 us -> 2.22 us
    all_gather x1 -> x0, blocking collectives: 32.8 us -> none  [body(): columns = lax.all_gather(col_factor, 'row', axis=0, tiled=True)]
    ppermute x0 -> x3, starting transfers between devices: none -> 8.3 us  [doubled(): other = lax.ppermute(blocks, axis, [(i, i ^ bit) for i in range(count)])]
    dot_general x1, matrix products: 14.9 us -> 19 us  [body(): inner = jnp.dot(flat, columns, preferred_element_type=jnp.float32)]
    slice x1, local copies, waits for them, and re-layouts: 0.57 us -> 3.99 us  [reduce_inner(): block = inner[start:start + 8]]
    slice x1 -> x9, local copies, waits for them, and re-layouts: 0.8 us -> 4.09 us  [reduce_inner(): aux_panel[start:start + 8][:, None, :]]
    ppermute x0 -> x3, waiting for transfers between devices: none -> 2.2 us  [doubled(): other = lax.ppermute(blocks, axis, [(i, i ^ bit) for i in range(count)])]
    reduce_sum x4, other arithmetic: 0.64 us -> 2.6 us  [reduce_inner(): jnp.sum(block * aux_panel[start:start + 8][:, None, :], axis=0)]
    unnamed x15 -> x29, local copies, waits for them, and re-layouts: 3.83 us -> 5.58 us
  transfers between devices with their start and end apart: 1 -> 4, of which waited for: 0 -> 2; matrix products, arithmetic and copies ran while one was open for 5% -> 10% of each run, Pallas kernels for 0% -> 0%
where the time goes in v1:
time: 110 us
  blocking collectives  41.5 us (38%)
  matrix products  19 us (17%)
  local copies, waits for them, and re-layouts  15 us (14%)
  between operations  15 us (14%)
  other arithmetic  8.59 us (8%)
  starting transfers between devices  8.34 us (8%)
  waiting for transfers between devices  2.22 us (2%)
    unnamed x1, blocking collectives  36.4 us
    dot_general x1, matrix products, body(): inner = jnp.dot(flat, columns, preferred_element_type=jnp.float32)  19 us
    ppermute x3, starting transfers between devices, doubled(): other = lax.ppermute(blocks, axis, [(i, i ^ bit) for i in range(count)])  8.3 us
    unnamed x29, local copies, waits for them, and re-layouts  5.58 us
    reduce_sum x1, other arithmetic, reduce_inner(): pieces.append(jnp.sum(block * row_panel[None, :, :], axis=1))  4.36 us
    slice x9, local copies, waits for them, and re-layouts, reduce_inner(): aux_panel[start:start + 8][:, None, :]  4.09 us
    slice x1, local copies, waits for them, and re-layouts, reduce_inner(): block = inner[start:start + 8]  3.99 us
    psum x1, blocking collectives, body(): aux_result = lax.psum(scattered, 'col')  3.04 us
  transfers between devices with their start and end apart: 4, of which 2 were waited for; matrix products, arithmetic and copies ran while one was open for 10% of the time, Pallas kernels for 0%

profile of v1, /device:TPU:0, one launch (start us, length us, event | category | flops | bytes accessed | tf_op | source)
XLA Modules:
  0.0 109.6 jit_solution(4599304864939741165)
XLA Ops:
  7.2 0.0 reduce-scatter.2.cloned.1.call-start
  7.2 3.0 %collective-permute-start = (bf16[1,128,128]{2,1,0:T(8,128)(2,1)}, bf16[1,128,128]{2,1,0:T(8,128)(2,1)S(1)}, u32[]{:S(2)}, u32[]{:S(2)}) collective-permute-start(bf16[1,128,128]{2,1,0:T(8,128)(2,1)} %bitcast.80), channel_id=1, source_target_pairs={{0,4},{4,0},{8,12},{12,8},{16,20},{20,16},{24,28},{28,24},{1,5},{5... | collective-permute-start | bytes 98312 | tf_op jit(solution)/shard_map/ppermute | solution.py:18
  10.2 2.1 %collective-permute-done = bf16[1,128,128]{2,1,0:T(8,128)(2,1)S(1)} collective-permute-done((bf16[1,128,128]{2,1,0:T(8,128)(2,1)}, bf16[1,128,128]{2,1,0:T(8,128)(2,1)S(1)}, u32[]{:S(2)}, u32[]{:S(2)}) %collective-permute-start) | collective-permute-done | bytes 32800 | tf_op jit(solution)/shard_map/ppermute | solution.py:18
  12.3 0.8 pad_maximum_fusion.2
  13.1 2.2 %collective-permute-start.1 = (bf16[2,128,128]{2,1,0:T(8,128)(2,1)S(1)}, bf16[2,128,128]{2,1,0:T(8,128)(2,1)S(1)}, u32[]{:S(2)}, u32[]{:S(2)}) collective-permute-start(bf16[2,128,128]{2,1,0:T(8,128)(2,1)S(1)} %get-tuple-element.21), channel_id=1, source_target_pairs={{0,8},{4,12},{8,0},{12,4},{16,24},{20,28},{24,16},{28,20},{1,9},{5... | collective-permute-start | bytes 196616 | tf_op jit(solution)/shard_map/ppermute | solution.py:18
  15.3 2.1 %all_gather.3 = bf16[256,128]{1,0:T(8,128)(2,1)S(1)} all-gather(bf16[128,128]{1,0:T(8,128)(2,1)} %param.6), channel_id=1, replica_groups=mesh['row'=8,'col'=2,'rank'=2] {'col'}, dimensions={0}, use_global_device_ids=true | all-gather | bytes 98304 | tf_op jit(solution)/shard_map/all_gather | solution.py:42
  17.4 0.1 copy.23
  17.5 0.1 collective-permute-done.1
  17.6 3.1 %collective-permute-start.2 = (bf16[4,128,128]{2,1,0:T(8,128)(2,1)S(1)}, bf16[4,128,128]{2,1,0:T(8,128)(2,1)S(1)}, u32[]{:S(2)}, u32[]{:S(2)}) collective-permute-start(bf16[4,128,128]{2,1,0:T(8,128)(2,1)S(1)} %bitcast.76), channel_id=1, source_target_pairs={{0,16},{4,20},{8,24},{12,28},{16,0},{20,4},{24,8},{28,12},{1,17},{... | collective-permute-start | bytes 393224 | tf_op jit(solution)/shard_map/ppermute | solution.py:18
  20.7 0.8 fusion.3
  21.5 0.7 copy.15
  22.2 0.7 copy.16
  22.9 0.1 copy.17
  23.0 0.7 copy.18
  23.8 0.1 copy.19
  23.9 0.1 copy.20
  24.0 0.1 copy.21
  24.1 0.7 copy.22
  24.8 1.2 %dynamic-slice = u32[1]{0:T(128)} dynamic-slice(u32[32]{0:T(128)} %constant.16, u32[]{:T(128)S(6)} %add.35), dynamic_slice_sizes={1} | dynamic-slice | bytes 12
  26.7 0.0 collective-permute-done.2
  26.7 0.1 reverse_select_fusion
  26.8 0.0 copy-start.6
  26.8 0.0 copy-start.8
  26.8 0.0 copy-start.7
  26.8 0.0 copy-start.5
  26.9 19.0 %convolution_bitcast_fusion = f32[16384,128]{0,1:T(8,128)} fusion(bf16[1024,128]{1,0:T(8,128)(2,1)S(1)} %bitcast.75, bf16[16384,1024]{1,0:T(8,128)(2,1)} %bitcast.58), kind=kOutput, calls=%fused_computation | convolution fusion | flops 4294967296 | bytes 42205184 | tf_op jit(solution)/shard_map/dot_general | solution.py:48
  45.9 4.0 %fusion.2 = (f32[2048,128]{0,1:T(8,128)S(1)}, f32[2048,128]{0,1:T(8,128)S(1)}, f32[2048,128]{0,1:T(8,128)S(1)}, f32[2048,128]{0,1:T(8,128)S(1)}, f32[2048,128]{0...) fusion(f32[16384,128]{0,1:T(8,128)} %convolution_bitcast_fusion), kind=kLoop, calls=%fused_computation.27 | loop fusion | bytes 16777216 | tf_op jit(solution)/shard_map/slice | solution.py:35
  49.9 0.3 copy.26
  50.2 0.3 copy.27
  50.6 0.3 copy.28
  50.9 0.3 copy.29
  51.3 0.0 copy-start
  51.3 0.3 copy.30
  51.6 0.0 copy-start.1
  51.6 0.3 copy.31
  52.0 0.0 copy-start.2
  52.0 0.3 copy.32
  52.3 0.0 copy-start.3
  52.4 0.3 copy.33
  52.7 0.0 copy-done.6
  52.7 0.0 copy-done.8
  52.7 0.0 copy-start.4
  52.7 0.7 multiply_reduce_fusion.14
  53.4 0.0 copy-done
  53.4 0.0 copy-done.7
  53.4 0.7 multiply_reduce_fusion.12
  54.1 0.0 copy-done.1
  54.1 0.6 multiply_reduce_fusion.10
  54.8 0.0 copy-done.2
  54.8 0.0 copy-done.5
  54.8 0.6 multiply_reduce_fusion.8
  55.4 0.0 copy-done.3
  55.4 0.0 copy-done.4
  55.4 0.7 add_add_fusion
  56.1 0.0 reduce-scatter.2.cloned.1.call-update
  56.2 4.4 %multiply_reduce_fusion = (f32[8,128]{0,1:T(8,128)S(1)}, f32[8,128]{0,1:T(8,128)S(1)}, f32[8,128]{0,1:T(8,128)S(1)}, f32[8,128]{0,1:T(8,128)S(1)}, f32[8,128]{0,...) fusion(f32[8,256,128]{1,0,2:T(8,128)} %bitcast.66, f32[256,128]{0,1:T(8,128)S(1)} %copy.23, ...), kind=kLoop, calls=%fused_computation.1 | loop fusion | flops 4186112 | bytes 8552448 | tf_op jit(solution)/shard_map/reduce_sum | solution.py:37
  60.5 1.1 %concatenate.3 = f32[64,128]{0,1:T(8,128)S(1)} concatenate(f32[8,128]{0,1:T(8,128)} %get-tuple-element.11, f32[8,128]{0,1:T(8,128)S(1)} %get-tuple-element.5, f32[8,128]{0,1:T(8,128)S(1)} %get-tuple-element.6, f32[8,128]{0,1:T(8,128)S(1)} %get-tuple-element.7, f32[8,128]{0,1:T(8,128)} %get-tuple-element.8, f32[8,128]{0,1:T(8,128)} %get-tuple-element.9, ...), dimensions={0} | concatenate | bytes 65536 | tf_op jit(solution)/shard_map/concatenate | solution.py:38
  61.7 0.1 copy.24
  61.7 36.4 %all-reduce = f32[64,128]{1,0:T(8,128)S(1)} all-reduce(f32[64,128]{1,0:T(8,128)S(1)} %copy.24), channel_id=3, replica_groups=mesh['row'=8,'col'=2,'rank'=2] {'row'}, use_global_device_ids=true, to_apply=%region_17.18.clone | all-reduce | flops 8192 | bytes 65536
  98.2 3.0 %psum.7 = f32[8,128]{1,0:T(8,128)} all-reduce(f32[8,128]{1,0:T(8,128)S(1)} %constant_dynamic-slice_fusion), channel_id=1, replica_groups=mesh['row'=8,'col'=2,'rank'=2] {'col'}, use_global_device_ids=true, to_apply=%region_18.19 | all-reduce | flops 1024 | bytes 8192 | tf_op jit(solution)/shard_map/psum | solution.py:53
  101.2 0.0 reduce-scatter.2.cloned.1.call-done
  101.2 1.6 %copy.25 = f32[128,128]{1,0:T(8,128)} copy(f32[128,128]{0,1:T(8,128)} %reduce-scatter.2.cloned.1.call-done) | data formatting | bytes 131072
  (5 shorter events, 0.1 us)
Async XLA Ops:
  7.2 94.0 %reduce-scatter.2.cloned.1.call-start = ((), (), s32[]{:S(2)}) async-start(), calls=%async_computation.1 | async-start | bytes 196608 | tf_op jit(solution)/shard_map/reduce_scatter | solution.py:51
  7.2 5.1 %collective-permute-start = (bf16[1,128,128]{2,1,0:T(8,128)(2,1)}, bf16[1,128,128]{2,1,0:T(8,128)(2,1)S(1)}, u32[]{:S(2)}, u32[]{:S(2)}) collective-permute-start(bf16[1,128,128]{2,1,0:T(8,128)(2,1)} %bitcast.80), channel_id=1, source_target_pairs={{0,4},{4,0},{8,12},{12,8},{16,20},{20,16},{24,28},{28,24},{1,5},{5... | collective-permute-start | bytes 98312 | tf_op jit(solution)/shard_map/ppermute | solution.py:18
  13.1 4.4 %collective-permute-start.1 = (bf16[2,128,128]{2,1,0:T(8,128)(2,1)S(1)}, bf16[2,128,128]{2,1,0:T(8,128)(2,1)S(1)}, u32[]{:S(2)}, u32[]{:S(2)}) collective-permute-start(bf16[2,128,128]{2,1,0:T(8,128)(2,1)S(1)} %get-tuple-element.21), channel_id=1, source_target_pairs={{0,8},{4,12},{8,0},{12,4},{16,24},{20,28},{24,16},{28,20},{1,9},{5... | collective-permute-start | bytes 196616 | tf_op jit(solution)/shard_map/ppermute | solution.py:18
  17.6 9.1 %collective-permute-start.2 = (bf16[4,128,128]{2,1,0:T(8,128)(2,1)S(1)}, bf16[4,128,128]{2,1,0:T(8,128)(2,1)S(1)}, u32[]{:S(2)}, u32[]{:S(2)}) collective-permute-start(bf16[4,128,128]{2,1,0:T(8,128)(2,1)S(1)} %bitcast.76), channel_id=1, source_target_pairs={{0,16},{4,20},{8,24},{12,28},{16,0},{20,4},{24,8},{28,12},{1,17},{... | collective-permute-start | bytes 393224 | tf_op jit(solution)/shard_map/ppermute | solution.py:18
  26.8 25.9 %copy-start.6 = (f32[8,128]{0,1:T(8,128)S(1)}, f32[8,128]{0,1:T(8,128)}, u32[]{:S(2)}) copy-start(f32[8,128]{0,1:T(8,128)} %copy.15) | copy-start | bytes 12292
  26.8 25.9 %copy-start.8 = (f32[8,128]{0,1:T(8,128)S(1)}, f32[8,128]{0,1:T(8,128)}, u32[]{:S(2)}) copy-start(f32[8,128]{0,1:T(8,128)} %copy.16) | copy-start | bytes 12292
  26.8 26.6 %copy-start.7 = (f32[8,128]{0,1:T(8,128)S(1)}, f32[8,128]{0,1:T(8,128)}, u32[]{:S(2)}) copy-start(f32[8,128]{0,1:T(8,128)} %copy.18) | copy-start | bytes 12292
  26.8 27.9 %copy-start.5 = (f32[8,128]{0,1:T(8,128)S(1)}, f32[8,128]{0,1:T(8,128)}, u32[]{:S(2)}) copy-start(f32[8,128]{0,1:T(8,128)} %copy.22) | copy-start | bytes 12292
  51.3 2.1 %copy-start = (f32[16,8,8,256]{3,2,1,0:T(8,128)}, f32[16,8,8,256]{3,2,1,0:T(8,128)S(1)}, u32[]{:S(2)}) copy-start(f32[16,8,8,256]{3,2,1,0:T(8,128)S(1)} %copy.29) | copy-start | bytes 3145732
  51.6 2.5 %copy-start.1 = (f32[16,8,8,256]{3,2,1,0:T(8,128)}, f32[16,8,8,256]{3,2,1,0:T(8,128)S(1)}, u32[]{:S(2)}) copy-start(f32[16,8,8,256]{3,2,1,0:T(8,128)S(1)} %copy.30) | copy-start | bytes 3145732
  52.0 2.8 %copy-start.2 = (f32[16,8,8,256]{3,2,1,0:T(8,128)}, f32[16,8,8,256]{3,2,1,0:T(8,128)S(1)}, u32[]{:S(2)}) copy-start(f32[16,8,8,256]{3,2,1,0:T(8,128)S(1)} %copy.31) | copy-start | bytes 3145732
  52.3 3.1 %copy-start.3 = (f32[16,8,8,256]{3,2,1,0:T(8,128)}, f32[16,8,8,256]{3,2,1,0:T(8,128)S(1)}, u32[]{:S(2)}) copy-start(f32[16,8,8,256]{3,2,1,0:T(8,128)S(1)} %copy.32) | copy-start | bytes 3145732
  52.7 2.7 %copy-start.4 = (f32[16,8,8,256]{3,2,1,0:T(8,128)}, f32[16,8,8,256]{3,2,1,0:T(8,128)S(1)}, u32[]{:S(2)}) copy-start(f32[16,8,8,256]{3,2,1,0:T(8,128)S(1)} %copy.33) | copy-start | bytes 3145732
Sparse Core Ops, SparseCore 0:
  56.3 7.8 reduce-scatter.1
